TPU v7x, 32 devices: a whole 2x2x4 slice. The times are simulated.
32 devices in a mesh: track: 4 (over y, x), tm: 8 (over z, core).
Axes of the slice: x: 2, y: 2, z: 4, core: 2. Of those that a mesh axis runs over, the one named last changes fastest.
Arguments:
- observations: float32 [1024, 16, 128], P('tm', 'track'), may hold values from -18 to 18
- dynamics: bfloat16 [256, 128, 128], P('track'), may hold values from -1 to 1
- smoother_gain: bfloat16 [256, 128, 128], P('track'), may hold values from -1 to 1
- gains: bfloat16 [256, 128], P('track'), may hold values from 0 to 1
- regime: int32 [256], P('tm'), may hold values from 0 to 255
Outputs:
- smoothed: float32 [1024, 16, 128], P('tm', 'track')
All inputs are finite; a program needn't handle non-finite values.
Results may differ from a plain program's by a relative error of at most 0.0003.
Values may be sent and summed in bfloat16 or wider, within the bound.
No kernel may reach another device: no remote copies, remote signals or barrier semaphores. Data moves between devices by JAX's collectives and lax.ppermute only.
A program may use at most 64 MiB of HBM per device.

v0:
```python
import functools

import jax
import jax.numpy as jnp
from jax import lax
from jax.experimental import pallas as pl
from jax.experimental.pallas import tpu as pltpu
from jax.sharding import PartitionSpec as P


F32 = jnp.float32
BF16 = jnp.bfloat16
VMEM = pl.BlockSpec(memory_space=pltpu.VMEM)
SMEM = pl.BlockSpec(memory_space=pltpu.SMEM)
HBM = pl.BlockSpec(memory_space=pltpu.HBM)
GRANT = 16 * 1024 * 1024


def call(kernel, outs, ins, cost, scratch=(), places=None):
    return pl.pallas_call(
        kernel,
        out_shape=outs,
        in_specs=ins,
        out_specs=places or [VMEM] * len(outs),
        scratch_shapes=list(scratch),
        compiler_params=pltpu.CompilerParams(vmem_limit_bytes=GRANT),
        cost_estimate=pl.CostEstimate(flops=cost, bytes_accessed=cost // 64, transcendentals=0),
    )


def shape(dims, dtype=F32):
    return jax.ShapeDtypeStruct(dims, dtype)


def split(value):
    high = value.astype(BF16)
    low = (value - high.astype(F32)).astype(BF16)
    return high, low


def times_rows(value, doubled):
    pieces = jnp.concatenate(split(value), axis=1)
    return lax.dot_general(
        pieces, doubled, (((1,), (1,)), ((), ())), preferred_element_type=F32
    )


def times(value, matrix):
    high, low = split(value)
    upper, lower = split(matrix)
    left = jnp.concatenate([high, low, high], axis=1)
    right = jnp.concatenate([upper, upper, lower], axis=0)
    return jnp.dot(left, right, preferred_element_type=F32)


def compose(first, second):
    width = first.shape[1]
    product = times(first, second[:width])
    return jnp.concatenate([product[:width], product[width:] + second[width:]], axis=0)


def apply(state, chart):
    width = chart.shape[1]
    return times(state, chart[:width]) + chart[width:]


def unit_matrix(width):
    rows = lax.broadcasted_iota(jnp.int32, (width, width), 0)
    return (rows == lax.broadcasted_iota(jnp.int32, (width, width), 1)).astype(F32)


def unit_chart(width, rows):
    return jnp.concatenate([unit_matrix(width), jnp.zeros((rows, width), F32)], axis=0)


def choose(index, options):
    value = options[0]
    for j in range(1, len(options)):
        value = jnp.where(index == j, options[j], value)
    return value


def swapped(rows, mask, groups):
    block = rows.shape[0] // groups
    return jnp.concatenate(
        [rows[(j ^ mask) * block : ((j ^ mask) + 1) * block] for j in range(groups)], axis=0
    )


def doubled(matrix):
    return jnp.concatenate([matrix, matrix], axis=1)


def step_rows(parts, t):
    return jnp.concatenate([part[t] for part in parts], axis=0)


class Plan:
    def __init__(self, groups, share, dwell, owned, tracks, width):
        self.groups, self.share, self.dwell = groups, share, dwell
        self.owned, self.tracks, self.width = owned, tracks, width
        self.span, self.rows = share * dwell, groups * tracks
        self.padded = -(-share // 16) * 16
        self.spare = share // 4
        self.fast = share - self.spare

    def local(self, regime_ref, peer, b):
        return regime_ref[peer * self.share + b] - lax.axis_index("track") * self.owned

    def here(self, regime_ref, peer, b):
        return jnp.clip(self.local(regime_ref, peer, b), 0, self.owned - 1)

    def source(self, regime_ref, b):
        me = lax.axis_index("track")
        return (regime_ref[me * self.share + b] // self.owned) ^ me

    def forward_steps(self):
        return [(b, b * self.dwell + i) for i in range(self.dwell) for b in range(self.share)]

    def backward_steps(self):
        turn = self.dwell - 1
        return [(b, t + turn - 2 * (t % self.dwell)) for b, t in self.forward_steps()]


def block_of(plan, ref, at):
    return ref.at[pl.ds(pl.multiple_of(at * plan.width, plan.width), plan.width)]


def each_row(plan, regime_ref, table_ref, targets, sem, act):
    def row(held, at, target):
        @pl.when(held)
        def _():
            copy = pltpu.make_async_copy(table_ref.at[at], target, sem)
            copy.start() if act else copy.wait()

    for j, main, more in targets:
        peer = lax.axis_index("track") ^ j
        slot = jnp.int32(0)
        for b in range(plan.share):
            at = plan.local(regime_ref, peer, b)
            held = jnp.logical_and(at >= 0, at < plan.owned)
            at = jnp.clip(at, 0, plan.owned - 1)
            if j == 0:
                row(held, at, block_of(plan, main, b))
                continue
            if b < plan.fast:
                row(held, at, block_of(plan, main, slot))
            else:
                fits = slot < plan.fast
                room = jnp.minimum(slot, plan.fast - 1)
                row(jnp.logical_and(held, fits), at, block_of(plan, main, room))
                late = jnp.clip(slot - plan.fast, 0, plan.spare - 1)
                row(jnp.logical_and(held, jnp.logical_not(fits)), at, block_of(plan, more, late))
            slot = slot + held.astype(jnp.int32)


def remote_targets(plan, refs):
    peers = plan.groups - 1
    return [(j + 1, refs[j], refs[peers + j]) for j in range(peers)]


def gather_kernel(plan, regime_ref, table_ref, gains_ref, *refs):
    own_ref, refs, (gain_ref, sem) = (refs[0], refs[1:-2], refs[-2:])
    each_row(plan, regime_ref, table_ref, remote_targets(plan, refs), sem, True)
    gain_ref[...] = gains_ref[...].astype(F32)
    for j in range(plan.groups):
        peer = lax.axis_index("track") ^ j
        rows = [min(b, plan.share - 1) for b in range(plan.padded)]
        found = [gain_ref[pl.ds(plan.here(regime_ref, peer, b), 1), :] for b in range(plan.share)]
        tile = jnp.concatenate([found[b] for b in rows], axis=0).astype(BF16)
        if j:
            refs[j - 1][plan.fast * plan.width :] = tile
        else:
            own_ref[...] = tile
    each_row(plan, regime_ref, table_ref, remote_targets(plan, refs), sem, False)


def second_gather_kernel(plan, regime_ref, first_ref, second_ref, *refs):
    over_ref, own_first, own_second, refs, sem = (*refs[:3], refs[3:-1], refs[-1])
    targets = [(0, own_second, None)] + remote_targets(plan, refs)
    for act in (True, False):
        each_row(plan, regime_ref, first_ref, [(0, own_first, None)], sem, act)
        each_row(plan, regime_ref, second_ref, targets, sem, act)
        if act:
            over_ref[0] = most_slots(plan, regime_ref)


def picked_matrix(plan, regime_ref, refs, b):
    peers = plan.groups - 1
    own, main, more = (refs[0], refs[1 : peers + 1], refs[peers + 1 :])
    me = lax.axis_index("track")
    holder = [lax.div(regime_ref[me * plan.share + i], plan.owned) for i in range(b + 1)]
    slot = sum((holder[i] == holder[b]).astype(jnp.int32) for i in range(b)) if b else 0
    source = holder[b] ^ me
    mine = own[b * plan.width : (b + 1) * plan.width]
    if b < plan.fast:
        return choose(source, [mine] + [block_of(plan, part, slot)[...] for part in main])
    room = jnp.minimum(slot, plan.fast - 1)
    found = choose(source, [mine] + [block_of(plan, part, room)[...] for part in main])
    late = jnp.clip(slot - plan.fast, 0, plan.spare - 1)
    rest = choose(source, [mine] + [block_of(plan, part, late)[...] for part in more])
    return jnp.where(slot < plan.fast, found, rest)


def measured_kernel(plan, obs_ref, *refs):
    meas, sem = (refs[:-1], refs[-1])
    copies = []
    for j in range(plan.groups):
        first = pl.multiple_of((lax.axis_index("track") ^ j) * plan.span, plan.span)
        rows = obs_ref.at[pl.ds(first, plan.span)]
        copies.append(pltpu.make_async_copy(rows, meas[j], sem.at[j]))
    for copy in copies:
        copy.start()
    for copy in copies:
        copy.wait()


def most_slots(plan, regime_ref):
    most = jnp.int32(0)
    for peer in range(plan.groups):
        holder = [lax.div(regime_ref[peer * plan.share + b], plan.owned) for b in range(plan.share)]
        for q in range(plan.groups):
            if q != peer:
                most = jnp.maximum(most, sum((at == q).astype(jnp.int32) for at in holder))
    return most


def joined(charts):
    while len(charts) > 1:
        odd = charts[len(charts) // 2 * 2 :]
        charts = [compose(charts[i], charts[i + 1]) for i in range(0, len(charts) - 1, 2)] + odd
    return charts[0]


def running(charts):
    if len(charts) == 1:
        return charts
    pairs = running([compose(charts[i], charts[i + 1]) for i in range(0, len(charts) - 1, 2)])
    found = [charts[0]]
    for i in range(1, len(charts)):
        found.append(pairs[i // 2] if i % 2 else compose(pairs[i // 2 - 1], charts[i]))
    return found


def forward_kernel(plan, regime_ref, own_gain_ref, *refs):
    mats, (strand_ref, tree_ref, picked_ref, gain_ref) = (refs[:-4], refs[-4:])
    tiles = [own_gain_ref[...].astype(F32)]
    tiles += [part[plan.fast * plan.width :].astype(F32) for part in mats[1 : plan.groups]]
    weights, gains, states = ([], [], [])
    for b in range(plan.share):
        picked = picked_matrix(plan, regime_ref, mats, b)
        picked_ref[b] = picked
        weights.append(doubled(picked))
        source = plan.source(regime_ref, b)
        gains.append(choose(source, [tile[b : b + 1] for tile in tiles]))
        gain_ref[b : b + 1] = gains[b]
        states.append(picked.astype(F32).T * (1.0 - gains[b]))
    for b, t in plan.forward_steps():
        if t % plan.dwell > 0:
            states[b] = times_rows(states[b], weights[b]) * (1.0 - gains[b])
    for b in range(plan.share):
        strand_ref[b] = states[b]
    at = 0
    while len(states) > 1:
        states = [times(states[i], states[i + 1]) for i in range(0, len(states), 2)]
        for state in states:
            tree_ref[at] = state
            at += 1


def offset_kernel(plan, strand_ref, tree_ref, picked_ref, gain_ref, *refs):
    meas, (total_ref, offset_ref) = (refs[:-2], refs[-2:])
    gains = [gain_ref[b : b + 1] for b in range(plan.share)]
    weights = [doubled(picked_ref[b]) for b in range(plan.share)]
    states = [gains[b] * step_rows(meas, b * plan.dwell) for b in range(plan.share)]
    for b, t in plan.forward_steps():
        if t % plan.dwell > 0:
            moved = times_rows(states[b], weights[b]) * (1.0 - gains[b])
            states[b] = moved + gains[b] * step_rows(meas, t)
    for b in range(plan.share):
        offset_ref[b] = states[b]
    mats = [strand_ref[b] for b in range(plan.share)]
    at = 0
    while len(states) > 1:
        pairs = range(0, len(states), 2)
        states = [times(states[i], mats[i + 1]) + states[i + 1] for i in pairs]
        mats = [tree_ref[at + i] for i in range(len(states))]
        at += len(states)
    total_ref[: plan.width] = mats[0]
    total_ref[plan.width :] = states[0]


def backward_kernel(plan, regime_ref, *refs):
    mats, (strand_ref, picked_ref) = (refs[:-2], refs[-2:])
    weights, states = ([], [])
    for b in range(plan.share):
        picked = picked_matrix(plan, regime_ref, mats, b)
        picked_ref[b] = picked
        weights.append(doubled(picked))
        states.append(picked.astype(F32).T)
    for b, t in plan.backward_steps():
        if t % plan.dwell < plan.dwell - 1:
            states[b] = times_rows(states[b], weights[b])
    for b in range(plan.share):
        strand_ref[b] = states[plan.share - 1 - b]


def running_kernel(strand_ref, offset_ref, running_ref):
    charts = [
        jnp.concatenate([strand_ref[s], offset_ref[s]], axis=0)
        for s in range(offset_ref.shape[0] - 1)
    ]
    for s, chart in enumerate(running(charts)):
        running_ref[s] = chart


def group_kernel(plan, reverse, *refs):
    groups, width = (plan.groups, plan.width)
    parts, (total_ref, before_ref) = (refs[:groups], refs[groups:])
    fixed = []
    for j in range(groups):
        part = parts[j][...]
        fixed.append(jnp.concatenate([part[:width], swapped(part[width:], j, groups)], axis=0))
    me = lax.axis_index("track")
    order = list(range(groups))[::-1] if reverse else list(range(groups))
    charts = [choose(me ^ q, fixed) for q in order]
    place = groups - 1 - me if reverse else me
    befores = [unit_chart(width, plan.rows), charts[0]]
    while len(befores) < groups:
        befores.append(compose(befores[-1], charts[len(befores) - 1]))
    before_ref[...] = choose(place, befores)
    total_ref[...] = joined(charts)


def is_second(mask, reverse):
    second = (lax.axis_index("tm") & mask) != 0
    return jnp.logical_not(second) if reverse else second


def pair_kernel(mask, reverse, own_ref, other_ref, before_ref, joined_ref, after_ref, *half_ref):
    own, other, before = (own_ref[...], other_ref[...], before_ref[...])
    second = is_second(mask, reverse)
    joined = compose(jnp.where(second, other, own), jnp.where(second, own, other))
    joined_ref[...] = joined
    after_ref[...] = jnp.where(second, compose(other, before), before)
    if half_ref:
        rows = joined.shape[0] // 2
        half_ref[0][...] = jnp.where(is_second(1, False), joined[rows:], joined[:rows])


def entering(found, running_ref, stride, reverse):
    before_ref, mine_ref, theirs_ref, half_ref, rest_ref = found
    odd = is_second(1, False)
    mine, theirs, half, rest = (mine_ref[...], theirs_ref[...], half_ref[...], rest_ref[...])
    across = jnp.concatenate([jnp.where(odd, rest, half), jnp.where(odd, half, rest)], axis=0)
    peers = [mine, jnp.where(odd, theirs, mine), jnp.where(odd, mine, theirs), across]
    low, high = (is_second(stride, False), is_second(2 * stride, False))
    quarter = low.astype(jnp.int32) + 2 * high.astype(jnp.int32)
    width = mine.shape[1]
    state = None
    for at in (3, 2, 1) if reverse else (0, 1, 2):
        chart = choose(quarter ^ at, peers)
        ahead = quarter < at if reverse else quarter > at
        if state is None:
            state = jnp.where(ahead, chart[width:], jnp.zeros_like(chart[width:]))
        else:
            state = jnp.where(ahead, apply(state, chart), state)
    state = apply(state, before_ref[...])
    return [state] + [apply(state, running_ref[s]) for s in range(running_ref.shape[0])]


def filter_kernel(plan, stride, *refs):
    found, (running_ref, fpick_ref, gain_ref), refs = (refs[:5], refs[5:8], refs[8:])
    meas, refs = (refs[: plan.groups], refs[plan.groups :])
    strand_ref, bpick_ref, filtered_ref, pushed_ref, offset_ref, total_ref = refs
    states = entering(found, running_ref, stride, False)
    gains = [gain_ref[b : b + 1] for b in range(plan.share)]
    weights = [doubled(fpick_ref[b]) for b in range(plan.share)]
    pushes = {}
    for b, t in plan.forward_steps():
        ahead = times_rows(states[b], weights[b])
        pushes[t] = gains[b] * (step_rows(meas, t) - ahead)
        states[b] = ahead + pushes[t]
        filtered_ref[t] = states[b]
        pushed_ref[t] = pushes[t]
    weights = [doubled(bpick_ref[b]) for b in range(plan.share)]
    states = [None] * plan.share
    for b, t in plan.backward_steps():
        state = pushes[t] if states[b] is None else states[b] + pushes[t]
        states[b] = times_rows(state, weights[b])
    states = states[::-1]
    for b in range(plan.share):
        offset_ref[b] = states[b]
    mats = [strand_ref[b] for b in range(plan.share)]
    while len(states) > 1:
        pairs = range(0, len(states), 2)
        states = [times(states[i], mats[i + 1]) + states[i + 1] for i in pairs]
        mats = [times(mats[i], mats[i + 1]) for i in pairs]
    total_ref[0 : plan.width] = mats[0]
    total_ref[plan.width :] = states[0]


def smooth_kernel(plan, stride, *refs):
    found, (running_ref, picked_ref, filtered_ref, pushed_ref), outs = (refs[:5], refs[5:9], refs[9:])
    tracks = plan.tracks
    states = entering(found, running_ref, stride, True)[::-1]
    weights = [doubled(picked_ref[b]) for b in range(plan.share)]
    for b, t in plan.backward_steps():
        value = filtered_ref[t] + states[b]
        for j in range(plan.groups):
            outs[j][t] = value[j * tracks : (j + 1) * tracks]
        if t % plan.dwell > 0:
            states[b] = times_rows(states[b] + pushed_ref[t], weights[b])


def collect_kernel(plan, *refs):
    parts, out_ref, sem = (refs[: plan.groups], refs[plan.groups], refs[plan.groups + 1])
    copies = []
    for j in range(plan.groups):
        first = pl.multiple_of((lax.axis_index("track") ^ j) * plan.span, plan.span)
        rows = out_ref.at[pl.ds(first, plan.span)]
        copies.append(pltpu.make_async_copy(parts[j], rows, sem.at[j]))
    for copy in copies:
        copy.start()
    for copy in copies:
        copy.wait()


def body(observations, dynamics, smoother_gain, gains, regime):
    length, tracks, width = observations.shape
    blocks = regime.shape[0]
    groups, spans = (lax.axis_size("track"), lax.axis_size("tm"))
    owned = dynamics.shape[0]
    plan = Plan(groups, blocks // groups, length // blocks, owned, tracks, width)
    chart = shape((width + plan.rows, width))
    offset = shape((plan.rows, width))
    half_chart = shape(((width + plan.rows) // 2, width))
    top = spans // 4
    share = plan.share
    block_mats = lambda count: shape((count, width, width), BF16)
    unit = width * width * width
    regime, observations, dynamics, smoother_gain, gains = [
        pltpu.with_memory_space_constraint(value, pltpu.HBM)
        for value in (regime, observations, dynamics, smoother_gain, gains)
    ]

    def swap(value, mask, axis):
        pairs = [(source, source ^ mask) for source in range(lax.axis_size(axis))]
        return lax.ppermute(value, axis, pairs)

    def exchange(values):
        found = [values[0]]
        for j in range(1, groups):
            found.append(swap(values[j], j, "track"))
        return found

    sem = pltpu.SemaphoreType.DMA
    peers = groups - 1
    rows_of = lambda rows: shape((rows, width), BF16)
    further_slots = [rows_of(plan.spare * width)] * peers
    slots = [rows_of(plan.fast * width)] * peers + further_slots
    gained = [rows_of(plan.fast * width + plan.padded)] * peers + further_slots
    own_gain, *trans = call(
        functools.partial(gather_kernel, plan),
        [rows_of(plan.padded)] + gained,
        [SMEM, HBM, VMEM],
        unit,
        [pltpu.VMEM((owned, width), F32), sem],
    )(regime, dynamics, gains)
    atrans = exchange([None, *trans[:peers]])[1:]
    meas = call(
        functools.partial(measured_kernel, plan),
        [shape((plan.span, tracks, width))] * groups,
        [HBM],
        unit,
        [sem((groups,))],
    )(observations)
    meas = exchange(meas)
    over, own, gown, *smooth = call(
        functools.partial(second_gather_kernel, plan),
        [shape((1,), jnp.int32)] + [rows_of(share * width)] * 2 + slots,
        [SMEM, HBM, HBM],
        unit,
        [sem],
        [SMEM] + [VMEM] * (2 + len(slots)),
    )(regime, dynamics, smoother_gain)

    def all_further(values):
        return [swap(value, j % peers + 1, "track") for j, value in enumerate(values)]

    further = lax.cond(
        over[0] > plan.fast, all_further, lambda values: values, [*trans[peers:], *smooth[peers:]]
    )
    squares = lambda count: shape((count, width, width))
    fstrand, ftree, fpick, gain_rows = call(
        functools.partial(forward_kernel, plan),
        [squares(share), squares(share - 1), block_mats(share), shape((share, width))],
        [SMEM] + [VMEM] * (2 * groups),
        300 * unit,
    )(regime, own_gain, own, *atrans, *further[:peers])
    total, foffset = call(
        functools.partial(offset_kernel, plan),
        [chart, shape((share,) + offset.shape)],
        [VMEM] * (4 + groups),
        100 * unit,
    )(fstrand, ftree, fpick, gain_rows, *meas)

    late = smooth[:peers]
    early = (0, 1)
    held, total = lax.optimization_barrier(([late[j] for j in range(peers) if j not in early], total))
    late = [late[j] if j in early else held.pop(0) for j in range(peers)]

    def spread(total):
        return exchange([total] * groups)

    def across(total, reverse):
        maps = spread(total)
        total, before = call(
            functools.partial(group_kernel, plan, reverse),
            [chart, chart],
            [VMEM] * groups,
            20 * unit,
        )(*maps)
        stride = 1
        while 4 * stride < spans:
            last = 8 * stride >= spans
            other = swap(total, stride, "tm")
            total, before, *half = call(
                functools.partial(pair_kernel, stride, reverse),
                [chart, chart] + [half_chart] * last,
                [VMEM] * 3,
                20 * unit,
            )(total, other, before)
            stride *= 2
        near = [(at, at ^ (stride << (at & 1))) for at in range(spans)]
        mine = lax.ppermute(total, "tm", near)
        half = swap(half[0], 3 * stride, "tm")
        theirs = swap(mine, 1, "tm")
        return before, mine, theirs, half, swap(half, 1, "tm")

    for j, value in enumerate(late):
        late[j] = swap(value, j + 1, "track")
    bstrand, bpick = call(
        functools.partial(backward_kernel, plan),
        [shape((share, width, width)), block_mats(share)],
        [SMEM] + [VMEM] * (2 * groups - 1),
        300 * unit,
    )(regime, gown, *late, *further[peers:])

    found = across(total, False)
    runs = [shape((share - 1,) + chart.shape)]
    (frun,) = call(running_kernel, runs, [VMEM] * 2, 60 * unit)(fstrand, foffset)
    filtered, pushed, offsets, total = call(
        functools.partial(filter_kernel, plan, top),
        [shape((plan.span, plan.rows, width))] * 2 + [shape((share,) + offset.shape), chart],
        [VMEM] * (10 + groups),
        100 * unit,
    )(*found, frun, fpick, gain_rows, *meas, bstrand, bpick)

    found = across(total, True)
    (brun,) = call(running_kernel, runs, [VMEM] * 2, 60 * unit)(bstrand, offsets)
    outs = call(
        functools.partial(smooth_kernel, plan, top),
        [shape((plan.span, tracks, width))] * groups,
        [VMEM] * 9,
        50 * unit,
    )(*found, brun, bpick, filtered, pushed)
    sent = exchange(outs)
    return call(
        functools.partial(collect_kernel, plan),
        [shape((length, tracks, width))],
        [VMEM] * groups,
        unit,
        [sem((groups,))],
        [HBM],
    )(*sent)[0]


def solution(mesh):
    placed = (
        P("tm", "track", None),
        P("track", None, None),
        P("track", None, None),
        P("track", None),
        P("tm"),
    )

    return jax.shard_map(
        body, mesh=mesh, in_specs=placed, out_specs=P("tm", "track", None), check_vma=False
    )
```

profile of v0, /device:TPU:0, one launch (start us, length us, event | category | flops | bytes accessed | tf_op | source)
XLA Modules:
  0.0 74.1 jit_solution(358995637925127958)
XLA Ops:
  0.0 2.2 %shard_map.55 = (s32[1]{0:T(128)}, bf16[1024,128]{1,0:T(8,128)(2,1)S(1)}, bf16[1024,128]{1,0:T(8,128)(2,1)S(1)}, bf16[768,128]{1,0:T(8,128)(2,1)S(1)}, bf16[768,...) custom-call(s32[32]{0:T(128)} %regime_ref.7, ...), custom_call_target="tpu_custom_call" | custom-call | flops 2097152 | bytes 32768 | tf_op jit(solution)/shard_map/pallas_call | solution.py:479
  2.2 1.7 %shard_map.56 = (bf16[16,128]{1,0:T(8,128)(2,1)S(1)}, bf16[784,128]{1,0:T(8,128)(2,1)S(1)}, bf16[784,128]{1,0:T(8,128)(2,1)S(1)}, bf16[784,128]{1,0:T(8,128)(2,1...) custom-call(s32[32]{0:T(128)} %regime_ref.7, ...), custom_call_target="tpu_custom_call" | custom-call | flops 2097152 | bytes 32768 | tf_op jit(solution)/shard_map/pallas_call | solution.py:463
  4.6 3.0 %collective-permute-start.6 = (bf16[784,128]{1,0:T(8,128)(2,1)S(1)}, bf16[784,128]{1,0:T(8,128)(2,1)S(1)}, u32[]{:S(2)}, u32[]{:S(2)}) collective-permute-start(bf16[784,128]{1,0:T(8,128)(2,1)S(1)} %get-tuple-element.92), channel_id=1, source_target_pairs={{0,8},{8,0},{16,24},{24,16},{1,9},{9,1},{17,25},{25,17},{2,10},{10... | collective-permute-start | bytes 602120 | tf_op jit(solution)/shard_map/ppermute | solution.py:449
  7.6 1.5 %collective-permute-start.7 = (bf16[784,128]{1,0:T(8,128)(2,1)S(1)}, bf16[784,128]{1,0:T(8,128)(2,1)S(1)}, u32[]{:S(2)}, u32[]{:S(2)}) collective-permute-start(bf16[784,128]{1,0:T(8,128)(2,1)S(1)} %get-tuple-element.93), channel_id=1, source_target_pairs={{0,16},{8,24},{16,0},{24,8},{1,17},{9,25},{17,1},{25,9},{2,18},{10... | collective-permute-start | bytes 602120 | tf_op jit(solution)/shard_map/ppermute | solution.py:449
  10.2 2.1 %collective-permute-start.10 = (f32[32,4,128]{2,1,0:T(4,128)S(1)}, f32[32,4,128]{2,1,0:T(4,128)S(1)}, u32[]{:S(2)}, u32[]{:S(2)}) collective-permute-start(f32[32,4,128]{2,1,0:T(4,128)S(1)} %get-tuple-element.111), channel_id=1, source_target_pairs={{0,16},{8,24},{16,0},{24,8},{1,17},{9,25},{17,1},{25,9},{2,18},{10... | collective-permute-start | bytes 196616 | tf_op jit(solution)/shard_map/ppermute | solution.py:449
  12.2 1.3 %collective-permute-start.11 = (f32[32,4,128]{2,1,0:T(4,128)S(1)}, f32[32,4,128]{2,1,0:T(4,128)S(1)}, u32[]{:S(2)}, u32[]{:S(2)}) collective-permute-start(f32[32,4,128]{2,1,0:T(4,128)S(1)} %get-tuple-element.112), channel_id=1, source_target_pairs={{0,24},{8,16},{16,8},{24,0},{1,25},{9,17},{17,9},{25,1},{2,26},{10... | collective-permute-start | bytes 196616 | tf_op jit(solution)/shard_map/ppermute | solution.py:449
  13.6 1.6 %collective-permute-start.9 = (f32[32,4,128]{2,1,0:T(4,128)S(1)}, f32[32,4,128]{2,1,0:T(4,128)S(1)}, u32[]{:S(2)}, u32[]{:S(2)}) collective-permute-start(f32[32,4,128]{2,1,0:T(4,128)S(1)} %get-tuple-element.110), channel_id=1, source_target_pairs={{0,8},{8,0},{16,24},{24,16},{1,9},{9,1},{17,25},{25,17},{2,10},{10... | collective-permute-start | bytes 196616 | tf_op jit(solution)/shard_map/ppermute | solution.py:449
  15.2 3.0 %collective-permute-done.7.refs_2_ = bf16[784,128]{1,0:T(8,128)(2,1)S(1)} collective-permute-done((bf16[784,128]{1,0:T(8,128)(2,1)S(1)}, bf16[784,128]{1,0:T(8,128)(2,1)S(1)}, u32[]{:S(2)}, u32[]{:S(2)}) %collective-permute-start.7) | collective-permute-done | bytes 200736 | tf_op jit(solution)/shard_map/ppermute | solution.py:449
  18.3 1.9 %shard_map.57 = (f32[8,128,128]{2,1,0:T(8,128)S(1)}, f32[7,128,128]{2,1,0:T(8,128)S(1)}, bf16[8,128,128]{2,1,0:T(8,128)(2,1)S(1)}, f32[8,128]{1,0:T(8,128)S(1)}) custom-call(s32[32]{0:T(128)} %regime_ref.7, bf16[16,128]{1,0:T(8,128)(2,1)S(1)} %get-tuple-element.90.own_gain_ref, bf16[1024,128]{1,0:T(8,128)(2,1)S(1)} %get-tuple-element.91.refs_0_, ...), custom_call_target="tpu_custom_call" | custom-call | flops 629145600 | bytes 9830400 | tf_op jit(solution)/shard_map/pallas_call | solution.py:495
  21.3 1.6 %collective-permute-start.13 = (f32[144,128]{1,0:T(8,128)S(1)}, f32[144,128]{1,0:T(8,128)S(1)}, u32[]{:S(2)}, u32[]{:S(2)}) collective-permute-start(f32[144,128]{1,0:T(8,128)S(1)} %get-tuple-element.114.refs_0_), channel_id=1, source_target_pairs={{0,16},{8,24},{16,0},{24,8},{1,17},{9,25},{17,1},{25,9},{2,18},{10... | collective-permute-start | bytes 221192 | tf_op jit(solution)/shard_map/ppermute | solution.py:449
  22.9 1.6 %collective-permute-start.14 = (f32[144,128]{1,0:T(8,128)S(1)}, f32[144,128]{1,0:T(8,128)S(1)}, u32[]{:S(2)}, u32[]{:S(2)}) collective-permute-start(f32[144,128]{1,0:T(8,128)S(1)} %get-tuple-element.114.refs_0_), channel_id=1, source_target_pairs={{0,24},{8,16},{16,8},{24,0},{1,25},{9,17},{17,9},{25,1},{2,26},{10... | collective-permute-start | bytes 221192 | tf_op jit(solution)/shard_map/ppermute | solution.py:449
  24.8 1.6 %collective-permute-start.21 = (bf16[768,128]{1,0:T(8,128)(2,1)S(1)}, bf16[768,128]{1,0:T(8,128)(2,1)S(1)}, u32[]{:S(2)}, u32[]{:S(2)}) collective-permute-start(bf16[768,128]{1,0:T(8,128)(2,1)S(1)} %get-tuple-element.123), channel_id=1, source_target_pairs={{0,16},{8,24},{16,0},{24,8},{1,17},{9,25},{17,1},{25,9},{2,18},{10... | collective-permute-start | bytes 589832 | tf_op jit(solution)/shard_map/ppermute | solution.py:449
  26.4 1.6 %collective-permute-start.22 = (bf16[768,128]{1,0:T(8,128)(2,1)S(1)}, bf16[768,128]{1,0:T(8,128)(2,1)S(1)}, u32[]{:S(2)}, u32[]{:S(2)}) collective-permute-start(bf16[768,128]{1,0:T(8,128)(2,1)S(1)} %get-tuple-element.124), channel_id=1, source_target_pairs={{0,24},{8,16},{16,8},{24,0},{1,25},{9,17},{17,9},{25,1},{2,26},{10... | collective-permute-start | bytes 589832 | tf_op jit(solution)/shard_map/ppermute | solution.py:449
  29.0 6.8 %collective-permute-start.15 = (f32[144,128]{1,0:T(8,128)S(1)}, f32[144,128]{1,0:T(8,128)S(1)}, u32[]{:S(2)}, u32[]{:S(2)}) collective-permute-start(f32[144,128]{1,0:T(8,128)S(1)} %get-tuple-element.115.own_ref), channel_id=1, source_target_pairs={{0,1},{1,0},{2,3},{3,2},{4,5},{5,4},{6,7},{7,6},{8,9},{9,8},{10,11... | collective-permute-start | bytes 221192 | tf_op jit(solution)/shard_map/ppermute | solution.py:449
  37.6 5.3 %collective-permute-done.16.refs_1_ = f32[144,128]{1,0:T(8,128)S(1)} collective-permute-done((f32[144,128]{1,0:T(8,128)S(1)}, f32[144,128]{1,0:T(8,128)S(1)}, u32[]{:S(2)}, u32[]{:S(2)}) %collective-permute-start.16) | collective-permute-done | bytes 73760 | tf_op jit(solution)/shard_map/ppermute | solution.py:536
  44.2 1.4 %shard_map.63 = (f32[8,128,128]{2,1,0:T(8,128)S(1)}, bf16[8,128,128]{2,1,0:T(8,128)(2,1)S(1)}) custom-call(s32[32]{0:T(128)} %regime_ref.7, bf16[1024,128]{1,0:T(8,128)(2,1)S(1)} %get-tuple-element.121.refs_0_, bf16[768,128]{1,0:T(8,128)(2,1)S(1)} %collective-permute-done.20.refs_1_, bf16[768,128]{1,0:T(8,128)(2,1)S(1)} %collective-permute-done.21.refs_2_, ...), custom_call_target="tpu_custom_call" | custom-call | flops 629145600 | bytes 9830400 | tf_op jit(solution)/shard_map/pallas_call | solution.py:543
  45.6 2.5 %shard_map.64 = (f32[32,16,128]{2,1,0:T(8,128)S(1)}, f32[32,16,128]{2,1,0:T(8,128)S(1)}, f32[8,16,128]{2,1,0:T(8,128)S(1)}, f32[144,128]{1,0:T(8,128)S(1)}) custom-call(f32[144,128]{1,0:T(8,128)S(1)} %get-tuple-element.117.refs_0_, f32[144,128]{1,0:T(8,128)S(1)} %collective-permute-done.16.refs_1_, f32[144,128]{1,0:T(8,128)S(1)} %collective-permute-done.17.refs_2_, ...), custom_call_target="tpu_custom_call" | custom-call | flops 209715200 | bytes 3276800 | tf_op jit(solution)/shard_map/pallas_call | solution.py:553
  50.2 1.5 %collective-permute-start.25 = (f32[144,128]{1,0:T(8,128)S(1)}, f32[144,128]{1,0:T(8,128)S(1)}, u32[]{:S(2)}, u32[]{:S(2)}) collective-permute-start(f32[144,128]{1,0:T(8,128)S(1)} %get-tuple-element.130.refs_0_), channel_id=1, source_target_pairs={{0,24},{8,16},{16,8},{24,0},{1,25},{9,17},{17,9},{25,1},{2,26},{10... | collective-permute-start | bytes 221192 | tf_op jit(solution)/shard_map/ppermute | solution.py:449
  52.6 1.5 %collective-permute-done.24.refs_2_ = f32[144,128]{1,0:T(8,128)S(1)} collective-permute-done((f32[144,128]{1,0:T(8,128)S(1)}, f32[144,128]{1,0:T(8,128)S(1)}, u32[]{:S(2)}, u32[]{:S(2)}) %collective-permute-start.24) | collective-permute-done | bytes 73760 | tf_op jit(solution)/shard_map/ppermute | solution.py:449
  54.1 1.3 %collective-permute-done.25.refs_3_ = f32[144,128]{1,0:T(8,128)S(1)} collective-permute-done((f32[144,128]{1,0:T(8,128)S(1)}, f32[144,128]{1,0:T(8,128)S(1)}, u32[]{:S(2)}, u32[]{:S(2)}) %collective-permute-start.25) | collective-permute-done | bytes 73760 | tf_op jit(solution)/shard_map/ppermute | solution.py:449
  57.6 1.5 %collective-permute-start.29 = (f32[72,128]{1,0:T(8,128)S(1)}, f32[72,128]{1,0:T(8,128)S(1)}, u32[]{:S(2)}, u32[]{:S(2)}) collective-permute-start(f32[72,128]{1,0:T(8,128)S(1)} %get-tuple-element.135), channel_id=1, source_target_pairs={{0,6},{1,7},{2,4},{3,5},{4,2},{5,3},{6,0},{7,1},{8,14},{9,15},{10,... | collective-permute-start | bytes 110600 | tf_op jit(solution)/shard_map/ppermute | solution.py:449
  59.2 4.4 %collective-permute-done.27.refs_1_ = f32[144,128]{1,0:T(8,128)S(1)} collective-permute-done((f32[144,128]{1,0:T(8,128)S(1)}, f32[144,128]{1,0:T(8,128)S(1)}, u32[]{:S(2)}, u32[]{:S(2)}) %collective-permute-start.27) | collective-permute-done | bytes 73760 | tf_op jit(solution)/shard_map/ppermute | solution.py:536
  68.2 1.4 %collective-permute-start.33 = (f32[32,4,128]{2,1,0:T(4,128)S(1)}, f32[32,4,128]{2,1,0:T(4,128)S(1)}, u32[]{:S(2)}, u32[]{:S(2)}) collective-permute-start(f32[32,4,128]{2,1,0:T(4,128)S(1)} %get-tuple-element.142), channel_id=1, source_target_pairs={{0,24},{8,16},{16,8},{24,0},{1,25},{9,17},{17,9},{25,1},{2,26},{10... | collective-permute-start | bytes 196616 | tf_op jit(solution)/shard_map/ppermute | solution.py:449
  71.2 2.2 %collective-permute-done.33.refs_3_ = f32[32,4,128]{2,1,0:T(4,128)S(1)} collective-permute-done((f32[32,4,128]{2,1,0:T(4,128)S(1)}, f32[32,4,128]{2,1,0:T(4,128)S(1)}, u32[]{:S(2)}, u32[]{:S(2)}) %collective-permute-start.33) | collective-permute-done | bytes 65568 | tf_op jit(solution)/shard_map/ppermute | solution.py:449
  (48 shorter events, 18.6 us)
Async XLA Ops:
  4.6 9.0 %collective-permute-start.6 = (bf16[784,128]{1,0:T(8,128)(2,1)S(1)}, bf16[784,128]{1,0:T(8,128)(2,1)S(1)}, u32[]{:S(2)}, u32[]{:S(2)}) collective-permute-start(bf16[784,128]{1,0:T(8,128)(2,1)S(1)} %get-tuple-element.92), channel_id=1, source_target_pairs={{0,8},{8,0},{16,24},{24,16},{1,9},{9,1},{17,25},{25,17},{2,10},{10... | collective-permute-start | bytes 602120 | tf_op jit(solution)/shard_map/ppermute | solution.py:449
  7.6 10.7 %collective-permute-start.7 = (bf16[784,128]{1,0:T(8,128)(2,1)S(1)}, bf16[784,128]{1,0:T(8,128)(2,1)S(1)}, u32[]{:S(2)}, u32[]{:S(2)}) collective-permute-start(bf16[784,128]{1,0:T(8,128)(2,1)S(1)} %get-tuple-element.93), channel_id=1, source_target_pairs={{0,16},{8,24},{16,0},{24,8},{1,17},{9,25},{17,1},{25,9},{2,18},{10... | collective-permute-start | bytes 602120 | tf_op jit(solution)/shard_map/ppermute | solution.py:449
  9.1 9.2 %collective-permute-start.8 = (bf16[784,128]{1,0:T(8,128)(2,1)S(1)}, bf16[784,128]{1,0:T(8,128)(2,1)S(1)}, u32[]{:S(2)}, u32[]{:S(2)}) collective-permute-start(bf16[784,128]{1,0:T(8,128)(2,1)S(1)} %get-tuple-element.94), channel_id=1, source_target_pairs={{0,24},{8,16},{16,8},{24,0},{1,25},{9,17},{17,9},{25,1},{2,26},{10... | collective-permute-start | bytes 602120 | tf_op jit(solution)/shard_map/ppermute | solution.py:449
  10.2 10.0 %collective-permute-start.10 = (f32[32,4,128]{2,1,0:T(4,128)S(1)}, f32[32,4,128]{2,1,0:T(4,128)S(1)}, u32[]{:S(2)}, u32[]{:S(2)}) collective-permute-start(f32[32,4,128]{2,1,0:T(4,128)S(1)} %get-tuple-element.111), channel_id=1, source_target_pairs={{0,16},{8,24},{16,0},{24,8},{1,17},{9,25},{17,1},{25,9},{2,18},{10... | collective-permute-start | bytes 196616 | tf_op jit(solution)/shard_map/ppermute | solution.py:449
  12.2 7.9 %collective-permute-start.11 = (f32[32,4,128]{2,1,0:T(4,128)S(1)}, f32[32,4,128]{2,1,0:T(4,128)S(1)}, u32[]{:S(2)}, u32[]{:S(2)}) collective-permute-start(f32[32,4,128]{2,1,0:T(4,128)S(1)} %get-tuple-element.112), channel_id=1, source_target_pairs={{0,24},{8,16},{16,8},{24,0},{1,25},{9,17},{17,9},{25,1},{2,26},{10... | collective-permute-start | bytes 196616 | tf_op jit(solution)/shard_map/ppermute | solution.py:449
  13.6 6.6 %collective-permute-start.9 = (f32[32,4,128]{2,1,0:T(4,128)S(1)}, f32[32,4,128]{2,1,0:T(4,128)S(1)}, u32[]{:S(2)}, u32[]{:S(2)}) collective-permute-start(f32[32,4,128]{2,1,0:T(4,128)S(1)} %get-tuple-element.110), channel_id=1, source_target_pairs={{0,8},{8,0},{16,24},{24,16},{1,9},{9,1},{17,25},{25,17},{2,10},{10... | collective-permute-start | bytes 196616 | tf_op jit(solution)/shard_map/ppermute | solution.py:449
  21.0 5.5 %collective-permute-start.12 = (f32[144,128]{1,0:T(8,128)S(1)}, f32[144,128]{1,0:T(8,128)S(1)}, u32[]{:S(2)}, u32[]{:S(2)}) collective-permute-start(f32[144,128]{1,0:T(8,128)S(1)} %get-tuple-element.114.refs_0_), channel_id=1, source_target_pairs={{0,8},{8,0},{16,24},{24,16},{1,9},{9,1},{17,25},{25,17},{2,10},{10... | collective-permute-start | bytes 221192 | tf_op jit(solution)/shard_map/ppermute | solution.py:449
  21.3 6.6 %collective-permute-start.13 = (f32[144,128]{1,0:T(8,128)S(1)}, f32[144,128]{1,0:T(8,128)S(1)}, u32[]{:S(2)}, u32[]{:S(2)}) collective-permute-start(f32[144,128]{1,0:T(8,128)S(1)} %get-tuple-element.114.refs_0_), channel_id=1, source_target_pairs={{0,16},{8,24},{16,0},{24,8},{1,17},{9,25},{17,1},{25,9},{2,18},{10... | collective-permute-start | bytes 221192 | tf_op jit(solution)/shard_map/ppermute | solution.py:449
  22.9 5.5 %collective-permute-start.14 = (f32[144,128]{1,0:T(8,128)S(1)}, f32[144,128]{1,0:T(8,128)S(1)}, u32[]{:S(2)}, u32[]{:S(2)}) collective-permute-start(f32[144,128]{1,0:T(8,128)S(1)} %get-tuple-element.114.refs_0_), channel_id=1, source_target_pairs={{0,24},{8,16},{16,8},{24,0},{1,25},{9,17},{17,9},{25,1},{2,26},{10... | collective-permute-start | bytes 221192 | tf_op jit(solution)/shard_map/ppermute | solution.py:449
  24.5 19.7 %collective-permute-start.20 = (bf16[768,128]{1,0:T(8,128)(2,1)S(1)}, bf16[768,128]{1,0:T(8,128)(2,1)S(1)}, u32[]{:S(2)}, u32[]{:S(2)}) collective-permute-start(bf16[768,128]{1,0:T(8,128)(2,1)S(1)} %get-tuple-element.122), channel_id=1, source_target_pairs={{0,8},{8,0},{16,24},{24,16},{1,9},{9,1},{17,25},{25,17},{2,10},{10... | collective-permute-start | bytes 589832 | tf_op jit(solution)/shard_map/ppermute | solution.py:449
  24.8 19.3 %collective-permute-start.21 = (bf16[768,128]{1,0:T(8,128)(2,1)S(1)}, bf16[768,128]{1,0:T(8,128)(2,1)S(1)}, u32[]{:S(2)}, u32[]{:S(2)}) collective-permute-start(bf16[768,128]{1,0:T(8,128)(2,1)S(1)} %get-tuple-element.123), channel_id=1, source_target_pairs={{0,16},{8,24},{16,0},{24,8},{1,17},{9,25},{17,1},{25,9},{2,18},{10... | collective-permute-start | bytes 589832 | tf_op jit(solution)/shard_map/ppermute | solution.py:449
  26.4 17.7 %collective-permute-start.22 = (bf16[768,128]{1,0:T(8,128)(2,1)S(1)}, bf16[768,128]{1,0:T(8,128)(2,1)S(1)}, u32[]{:S(2)}, u32[]{:S(2)}) collective-permute-start(bf16[768,128]{1,0:T(8,128)(2,1)S(1)} %get-tuple-element.124), channel_id=1, source_target_pairs={{0,24},{8,16},{16,8},{24,0},{1,25},{9,17},{17,9},{25,1},{2,26},{10... | collective-permute-start | bytes 589832 | tf_op jit(solution)/shard_map/ppermute | solution.py:449
  29.0 7.7 %collective-permute-start.15 = (f32[144,128]{1,0:T(8,128)S(1)}, f32[144,128]{1,0:T(8,128)S(1)}, u32[]{:S(2)}, u32[]{:S(2)}) collective-permute-start(f32[144,128]{1,0:T(8,128)S(1)} %get-tuple-element.115.own_ref), channel_id=1, source_target_pairs={{0,1},{1,0},{2,3},{3,2},{4,5},{5,4},{6,7},{7,6},{8,9},{9,8},{10,11... | collective-permute-start | bytes 221192 | tf_op jit(solution)/shard_map/ppermute | solution.py:449
  36.9 6.0 %collective-permute-start.16 = (f32[144,128]{1,0:T(8,128)S(1)}, f32[144,128]{1,0:T(8,128)S(1)}, u32[]{:S(2)}, u32[]{:S(2)}) collective-permute-start(f32[144,128]{1,0:T(8,128)S(1)} %get-tuple-element.118), channel_id=1, source_target_pairs={{0,2},{1,5},{2,0},{3,7},{4,6},{5,1},{6,4},{7,3},{8,10},{9,13},{10,... | collective-permute-start | bytes 221192 | tf_op jit(solution)/shard_map/ppermute | solution.py:536
  37.0 6.6 %collective-permute-start.18 = (f32[72,128]{1,0:T(8,128)S(1)}, f32[72,128]{1,0:T(8,128)S(1)}, u32[]{:S(2)}, u32[]{:S(2)}) collective-permute-start(f32[72,128]{1,0:T(8,128)S(1)} %get-tuple-element.119), channel_id=1, source_target_pairs={{0,6},{1,7},{2,4},{3,5},{4,2},{5,3},{6,0},{7,1},{8,14},{9,15},{10,... | collective-permute-start | bytes 110600 | tf_op jit(solution)/shard_map/ppermute | solution.py:449
  42.9 2.7 %collective-permute-start.17 = (f32[144,128]{1,0:T(8,128)S(1)}, f32[144,128]{1,0:T(8,128)S(1)}, u32[]{:S(2)}, u32[]{:S(2)}) collective-permute-start(f32[144,128]{1,0:T(8,128)S(1)} %collective-permute-done.16.refs_1_), channel_id=1, source_target_pairs={{0,1},{1,0},{2,3},{3,2},{4,5},{5,4},{6,7},{7,6},{8,9},{9,8},{10,11... | collective-permute-start | bytes 221192 | tf_op jit(solution)/shard_map/ppermute | solution.py:449
  48.2 4.5 %collective-permute-start.23 = (f32[144,128]{1,0:T(8,128)S(1)}, f32[144,128]{1,0:T(8,128)S(1)}, u32[]{:S(2)}, u32[]{:S(2)}) collective-permute-start(f32[144,128]{1,0:T(8,128)S(1)} %get-tuple-element.130.refs_0_), channel_id=1, source_target_pairs={{0,8},{8,0},{16,24},{24,16},{1,9},{9,1},{17,25},{25,17},{2,10},{10... | collective-permute-start | bytes 221192 | tf_op jit(solution)/shard_map/ppermute | solution.py:449
  49.0 5.1 %collective-permute-start.24 = (f32[144,128]{1,0:T(8,128)S(1)}, f32[144,128]{1,0:T(8,128)S(1)}, u32[]{:S(2)}, u32[]{:S(2)}) collective-permute-start(f32[144,128]{1,0:T(8,128)S(1)} %get-tuple-element.130.refs_0_), channel_id=1, source_target_pairs={{0,16},{8,24},{16,0},{24,8},{1,17},{9,25},{17,1},{25,9},{2,18},{10... | collective-permute-start | bytes 221192 | tf_op jit(solution)/shard_map/ppermute | solution.py:449
  50.2 5.3 %collective-permute-start.25 = (f32[144,128]{1,0:T(8,128)S(1)}, f32[144,128]{1,0:T(8,128)S(1)}, u32[]{:S(2)}, u32[]{:S(2)}) collective-permute-start(f32[144,128]{1,0:T(8,128)S(1)} %get-tuple-element.130.refs_0_), channel_id=1, source_target_pairs={{0,24},{8,16},{16,8},{24,0},{1,25},{9,17},{17,9},{25,1},{2,26},{10... | collective-permute-start | bytes 221192 | tf_op jit(solution)/shard_map/ppermute | solution.py:449
  57.6 6.0 %collective-permute-start.27 = (f32[144,128]{1,0:T(8,128)S(1)}, f32[144,128]{1,0:T(8,128)S(1)}, u32[]{:S(2)}, u32[]{:S(2)}) collective-permute-start(f32[144,128]{1,0:T(8,128)S(1)} %get-tuple-element.134), channel_id=1, source_target_pairs={{0,2},{1,5},{2,0},{3,7},{4,6},{5,1},{6,4},{7,3},{8,10},{9,13},{10,... | collective-permute-start | bytes 221192 | tf_op jit(solution)/shard_map/ppermute | solution.py:536
  57.6 5.9 %collective-permute-start.29 = (f32[72,128]{1,0:T(8,128)S(1)}, f32[72,128]{1,0:T(8,128)S(1)}, u32[]{:S(2)}, u32[]{:S(2)}) collective-permute-start(f32[72,128]{1,0:T(8,128)S(1)} %get-tuple-element.135), channel_id=1, source_target_pairs={{0,6},{1,7},{2,4},{3,5},{4,2},{5,3},{6,0},{7,1},{8,14},{9,15},{10,... | collective-permute-start | bytes 110600 | tf_op jit(solution)/shard_map/ppermute | solution.py:449
  66.1 4.4 %collective-permute-start.31 = (f32[32,4,128]{2,1,0:T(4,128)S(1)}, f32[32,4,128]{2,1,0:T(4,128)S(1)}, u32[]{:S(2)}, u32[]{:S(2)}) collective-permute-start(f32[32,4,128]{2,1,0:T(4,128)S(1)} %get-tuple-element.140), channel_id=1, source_target_pairs={{0,8},{8,0},{16,24},{24,16},{1,9},{9,1},{17,25},{25,17},{2,10},{10... | collective-permute-start | bytes 196616 | tf_op jit(solution)/shard_map/ppermute | solution.py:449
  66.9 4.3 %collective-permute-start.32 = (f32[32,4,128]{2,1,0:T(4,128)S(1)}, f32[32,4,128]{2,1,0:T(4,128)S(1)}, u32[]{:S(2)}, u32[]{:S(2)}) collective-permute-start(f32[32,4,128]{2,1,0:T(4,128)S(1)} %get-tuple-element.141), channel_id=1, source_target_pairs={{0,16},{8,24},{16,0},{24,8},{1,17},{9,25},{17,1},{25,9},{2,18},{10... | collective-permute-start | bytes 196616 | tf_op jit(solution)/shard_map/ppermute | solution.py:449
  68.2 5.2 %collective-permute-start.33 = (f32[32,4,128]{2,1,0:T(4,128)S(1)}, f32[32,4,128]{2,1,0:T(4,128)S(1)}, u32[]{:S(2)}, u32[]{:S(2)}) collective-permute-start(f32[32,4,128]{2,1,0:T(4,128)S(1)} %get-tuple-element.142), channel_id=1, source_target_pairs={{0,24},{8,16},{16,8},{24,0},{1,25},{9,17},{17,9},{25,1},{2,26},{10... | collective-permute-start | bytes 196616 | tf_op jit(solution)/shard_map/ppermute | solution.py:449
  (4 other events, 6.1 us)
where the time goes:
time: 74.5 us; the launch traced here: 74.1 us
  starting transfers between devices  34 us (46%)
  waiting for transfers between devices  23 us (31%)
  Pallas kernels  16.2 us (22%)
  between operations  0.84 us (1%)
    ppermute x26, starting transfers between devices, swap(): return lax.ppermute(value, axis, pairs)  33.9 us
    ppermute x26, waiting for transfers between devices, swap(): return lax.ppermute(value, axis, pairs)  13.4 us
    ppermute x2, waiting for transfers between devices, across(): mine = lax.ppermute(total, 'tm', near)  9.67 us
    pallas_call x1, Pallas kernels, body(): call(functools.partial(filter_kernel, plan, top), [shape((plan.span, plan...  2.52 us
    pallas_call x1, Pallas kernels, body(): call(functools.partial(second_gather_kernel, plan), [shape((1,), jnp.int3...  2.18 us
    pallas_call x1, Pallas kernels, body(): call(functools.partial(forward_kernel, plan), [squares(share), squares(sh...  1.88 us
    pallas_call x1, Pallas kernels, body(): call(functools.partial(gather_kernel, plan), [rows_of(plan.padded)] + gai...  1.72 us
  transfers between devices with their start and end apart: 28, of which 13 were waited for; matrix products, arithmetic and copies ran while one was open for 0% of the time, Pallas kernels for 9%

commit v1 on v0

--- a/solution.py
+++ b/solution.py
@@ -126,13 +126,13 @@
     return ref.at[pl.ds(pl.multiple_of(at * plan.width, plan.width), plan.width)]
 
 
-def each_row(plan, regime_ref, table_ref, targets, sem, act):
+def start_rows(plan, regime_ref, table_ref, targets, sem):
     def row(held, at, target):
         @pl.when(held)
         def _():
-            copy = pltpu.make_async_copy(table_ref.at[at], target, sem)
-            copy.start() if act else copy.wait()
-
+            pltpu.make_async_copy(table_ref.at[at], target, sem).start()
+
+    count = jnp.int32(0)
     for j, main, more in targets:
         peer = lax.axis_index("track") ^ j
         slot = jnp.int32(0)
@@ -140,6 +140,7 @@
             at = plan.local(regime_ref, peer, b)
             held = jnp.logical_and(at >= 0, at < plan.owned)
             at = jnp.clip(at, 0, plan.owned - 1)
+            count = count + held.astype(jnp.int32)
             if j == 0:
                 row(held, at, block_of(plan, main, b))
                 continue
@@ -152,6 +153,15 @@
                 late = jnp.clip(slot - plan.fast, 0, plan.spare - 1)
                 row(jnp.logical_and(held, jnp.logical_not(fits)), at, block_of(plan, more, late))
             slot = slot + held.astype(jnp.int32)
+    return count
+
+
+def await_rows(plan, table_ref, target_ref, sem, count):
+    def one(_, carry):
+        pltpu.make_async_copy(table_ref.at[0], block_of(plan, target_ref, 0), sem).wait()
+        return carry
+
+    lax.fori_loop(0, count, one, 0)
 
 
 def remote_targets(plan, refs):
@@ -161,7 +171,7 @@
 
 def gather_kernel(plan, regime_ref, table_ref, gains_ref, *refs):
     own_ref, refs, (gain_ref, sem) = (refs[0], refs[1:-2], refs[-2:])
-    each_row(plan, regime_ref, table_ref, remote_targets(plan, refs), sem, True)
+    count = start_rows(plan, regime_ref, table_ref, remote_targets(plan, refs), sem)
     gain_ref[...] = gains_ref[...].astype(F32)
     for j in range(plan.groups):
         peer = lax.axis_index("track") ^ j
@@ -172,17 +182,16 @@
             refs[j - 1][plan.fast * plan.width :] = tile
         else:
             own_ref[...] = tile
-    each_row(plan, regime_ref, table_ref, remote_targets(plan, refs), sem, False)
+    await_rows(plan, table_ref, refs[0], sem, count)
 
 
 def second_gather_kernel(plan, regime_ref, first_ref, second_ref, *refs):
     over_ref, own_first, own_second, refs, sem = (*refs[:3], refs[3:-1], refs[-1])
     targets = [(0, own_second, None)] + remote_targets(plan, refs)
-    for act in (True, False):
-        each_row(plan, regime_ref, first_ref, [(0, own_first, None)], sem, act)
-        each_row(plan, regime_ref, second_ref, targets, sem, act)
-        if act:
-            over_ref[0] = most_slots(plan, regime_ref)
+    count = start_rows(plan, regime_ref, first_ref, [(0, own_first, None)], sem)
+    count = count + start_rows(plan, regime_ref, second_ref, targets, sem)
+    over_ref[0] = most_slots(plan, regime_ref)
+    await_rows(plan, first_ref, own_first, sem, count)
 
 
 def picked_matrix(plan, regime_ref, refs, b):

time: 74.5 us -> 74.5 us (level)
  no operation moved by 1% of the time
where the time goes in v1:
time: 74.5 us; the launch traced here: 74.1 us
  starting transfers between devices  34 us (46%)
  waiting for transfers between devices  23 us (31%)
  Pallas kernels  16.2 us (22%)
  between operations  0.84 us (1%)
    ppermute x26, starting transfers between devices, swap(): return lax.ppermute(value, axis, pairs)  33.9 us
    ppermute x26, waiting for transfers between devices, swap(): return lax.ppermute(value, axis, pairs)  13.4 us
    ppermute x2, waiting for transfers between devices, across(): mine = lax.ppermute(total, 'tm', near)  9.65 us
    pallas_call x1, Pallas kernels, body(): call(functools.partial(filter_kernel, plan, top), [shape((plan.span, plan...  2.52 us
    pallas_call x1, Pallas kernels, body(): call(functools.partial(second_gather_kernel, plan), [shape((1,), jnp.int3...  2.2 us
    pallas_call x1, Pallas kernels, body(): call(functools.partial(forward_kernel, plan), [squares(share), squares(sh...  1.89 us
    pallas_call x1, Pallas kernels, body(): call(functools.partial(gather_kernel, plan), [rows_of(plan.padded)] + gai...  1.72 us
  transfers between devices with their start and end apart: 28, of which 13 were waited for; matrix products, arithmetic and copies ran while one was open for 0% of the time, Pallas kernels for 9%

profile of v1, /device:TPU:0, one launch (start us, length us, event | category | flops | bytes accessed | tf_op | source)
XLA Modules:
  0.0 74.1 jit_solution(13708938558213278890)
XLA Ops:
  0.0 2.2 %shard_map.55 = (s32[1]{0:T(128)}, bf16[1024,128]{1,0:T(8,128)(2,1)S(1)}, bf16[1024,128]{1,0:T(8,128)(2,1)S(1)}, bf16[768,128]{1,0:T(8,128)(2,1)S(1)}, bf16[768,...) custom-call(s32[32]{0:T(128)} %regime_ref.7, ...), custom_call_target="tpu_custom_call" | custom-call | flops 2097152 | bytes 32768 | tf_op jit(solution)/shard_map/pallas_call | solution.py:488
  2.2 1.7 %shard_map.56 = (bf16[16,128]{1,0:T(8,128)(2,1)S(1)}, bf16[784,128]{1,0:T(8,128)(2,1)S(1)}, bf16[784,128]{1,0:T(8,128)(2,1)S(1)}, bf16[784,128]{1,0:T(8,128)(2,1...) custom-call(s32[32]{0:T(128)} %regime_ref.7, ...), custom_call_target="tpu_custom_call" | custom-call | flops 2097152 | bytes 32768 | tf_op jit(solution)/shard_map/pallas_call | solution.py:472
  4.6 3.0 %collective-permute-start.6 = (bf16[784,128]{1,0:T(8,128)(2,1)S(1)}, bf16[784,128]{1,0:T(8,128)(2,1)S(1)}, u32[]{:S(2)}, u32[]{:S(2)}) collective-permute-start(bf16[784,128]{1,0:T(8,128)(2,1)S(1)} %get-tuple-element.92), channel_id=1, source_target_pairs={{0,8},{8,0},{16,24},{24,16},{1,9},{9,1},{17,25},{25,17},{2,10},{10... | collective-permute-start | bytes 602120 | tf_op jit(solution)/shard_map/ppermute | solution.py:458
  7.6 1.5 %collective-permute-start.7 = (bf16[784,128]{1,0:T(8,128)(2,1)S(1)}, bf16[784,128]{1,0:T(8,128)(2,1)S(1)}, u32[]{:S(2)}, u32[]{:S(2)}) collective-permute-start(bf16[784,128]{1,0:T(8,128)(2,1)S(1)} %get-tuple-element.93), channel_id=1, source_target_pairs={{0,16},{8,24},{16,0},{24,8},{1,17},{9,25},{17,1},{25,9},{2,18},{10... | collective-permute-start | bytes 602120 | tf_op jit(solution)/shard_map/ppermute | solution.py:458
  10.2 2.1 %collective-permute-start.10 = (f32[32,4,128]{2,1,0:T(4,128)S(1)}, f32[32,4,128]{2,1,0:T(4,128)S(1)}, u32[]{:S(2)}, u32[]{:S(2)}) collective-permute-start(f32[32,4,128]{2,1,0:T(4,128)S(1)} %get-tuple-element.111), channel_id=1, source_target_pairs={{0,16},{8,24},{16,0},{24,8},{1,17},{9,25},{17,1},{25,9},{2,18},{10... | collective-permute-start | bytes 196616 | tf_op jit(solution)/shard_map/ppermute | solution.py:458
  12.3 1.3 %collective-permute-start.11 = (f32[32,4,128]{2,1,0:T(4,128)S(1)}, f32[32,4,128]{2,1,0:T(4,128)S(1)}, u32[]{:S(2)}, u32[]{:S(2)}) collective-permute-start(f32[32,4,128]{2,1,0:T(4,128)S(1)} %get-tuple-element.112), channel_id=1, source_target_pairs={{0,24},{8,16},{16,8},{24,0},{1,25},{9,17},{17,9},{25,1},{2,26},{10... | collective-permute-start | bytes 196616 | tf_op jit(solution)/shard_map/ppermute | solution.py:458
  13.6 1.6 %collective-permute-start.9 = (f32[32,4,128]{2,1,0:T(4,128)S(1)}, f32[32,4,128]{2,1,0:T(4,128)S(1)}, u32[]{:S(2)}, u32[]{:S(2)}) collective-permute-start(f32[32,4,128]{2,1,0:T(4,128)S(1)} %get-tuple-element.110), channel_id=1, source_target_pairs={{0,8},{8,0},{16,24},{24,16},{1,9},{9,1},{17,25},{25,17},{2,10},{10... | collective-permute-start | bytes 196616 | tf_op jit(solution)/shard_map/ppermute | solution.py:458
  15.2 3.0 %collective-permute-done.7.refs_2_ = bf16[784,128]{1,0:T(8,128)(2,1)S(1)} collective-permute-done((bf16[784,128]{1,0:T(8,128)(2,1)S(1)}, bf16[784,128]{1,0:T(8,128)(2,1)S(1)}, u32[]{:S(2)}, u32[]{:S(2)}) %collective-permute-start.7) | collective-permute-done | bytes 200736 | tf_op jit(solution)/shard_map/ppermute | solution.py:458
  18.3 1.9 %shard_map.57 = (f32[8,128,128]{2,1,0:T(8,128)S(1)}, f32[7,128,128]{2,1,0:T(8,128)S(1)}, bf16[8,128,128]{2,1,0:T(8,128)(2,1)S(1)}, f32[8,128]{1,0:T(8,128)S(1)}) custom-call(s32[32]{0:T(128)} %regime_ref.7, bf16[16,128]{1,0:T(8,128)(2,1)S(1)} %get-tuple-element.90.own_gain_ref, bf16[1024,128]{1,0:T(8,128)(2,1)S(1)} %get-tuple-element.91.refs_0_, ...), custom_call_target="tpu_custom_call" | custom-call | flops 629145600 | bytes 9830400 | tf_op jit(solution)/shard_map/pallas_call | solution.py:504
  21.4 1.6 %collective-permute-start.13 = (f32[144,128]{1,0:T(8,128)S(1)}, f32[144,128]{1,0:T(8,128)S(1)}, u32[]{:S(2)}, u32[]{:S(2)}) collective-permute-start(f32[144,128]{1,0:T(8,128)S(1)} %get-tuple-element.114.refs_0_), channel_id=1, source_target_pairs={{0,16},{8,24},{16,0},{24,8},{1,17},{9,25},{17,1},{25,9},{2,18},{10... | collective-permute-start | bytes 221192 | tf_op jit(solution)/shard_map/ppermute | solution.py:458
  22.9 1.6 %collective-permute-start.14 = (f32[144,128]{1,0:T(8,128)S(1)}, f32[144,128]{1,0:T(8,128)S(1)}, u32[]{:S(2)}, u32[]{:S(2)}) collective-permute-start(f32[144,128]{1,0:T(8,128)S(1)} %get-tuple-element.114.refs_0_), channel_id=1, source_target_pairs={{0,24},{8,16},{16,8},{24,0},{1,25},{9,17},{17,9},{25,1},{2,26},{10... | collective-permute-start | bytes 221192 | tf_op jit(solution)/shard_map/ppermute | solution.py:458
  24.8 1.6 %collective-permute-start.21 = (bf16[768,128]{1,0:T(8,128)(2,1)S(1)}, bf16[768,128]{1,0:T(8,128)(2,1)S(1)}, u32[]{:S(2)}, u32[]{:S(2)}) collective-permute-start(bf16[768,128]{1,0:T(8,128)(2,1)S(1)} %get-tuple-element.123), channel_id=1, source_target_pairs={{0,16},{8,24},{16,0},{24,8},{1,17},{9,25},{17,1},{25,9},{2,18},{10... | collective-permute-start | bytes 589832 | tf_op jit(solution)/shard_map/ppermute | solution.py:458
  26.4 1.6 %collective-permute-start.22 = (bf16[768,128]{1,0:T(8,128)(2,1)S(1)}, bf16[768,128]{1,0:T(8,128)(2,1)S(1)}, u32[]{:S(2)}, u32[]{:S(2)}) collective-permute-start(bf16[768,128]{1,0:T(8,128)(2,1)S(1)} %get-tuple-element.124), channel_id=1, source_target_pairs={{0,24},{8,16},{16,8},{24,0},{1,25},{9,17},{17,9},{25,1},{2,26},{10... | collective-permute-start | bytes 589832 | tf_op jit(solution)/shard_map/ppermute | solution.py:458
  29.0 6.8 %collective-permute-start.15 = (f32[144,128]{1,0:T(8,128)S(1)}, f32[144,128]{1,0:T(8,128)S(1)}, u32[]{:S(2)}, u32[]{:S(2)}) collective-permute-start(f32[144,128]{1,0:T(8,128)S(1)} %get-tuple-element.115.own_ref), channel_id=1, source_target_pairs={{0,1},{1,0},{2,3},{3,2},{4,5},{5,4},{6,7},{7,6},{8,9},{9,8},{10,11... | collective-permute-start | bytes 221192 | tf_op jit(solution)/shard_map/ppermute | solution.py:458
  37.6 5.3 %collective-permute-done.16.refs_1_ = f32[144,128]{1,0:T(8,128)S(1)} collective-permute-done((f32[144,128]{1,0:T(8,128)S(1)}, f32[144,128]{1,0:T(8,128)S(1)}, u32[]{:S(2)}, u32[]{:S(2)}) %collective-permute-start.16) | collective-permute-done | bytes 73760 | tf_op jit(solution)/shard_map/ppermute | solution.py:545
  44.2 1.4 %shard_map.63 = (f32[8,128,128]{2,1,0:T(8,128)S(1)}, bf16[8,128,128]{2,1,0:T(8,128)(2,1)S(1)}) custom-call(s32[32]{0:T(128)} %regime_ref.7, bf16[1024,128]{1,0:T(8,128)(2,1)S(1)} %get-tuple-element.121.refs_0_, bf16[768,128]{1,0:T(8,128)(2,1)S(1)} %collective-permute-done.20.refs_1_, bf16[768,128]{1,0:T(8,128)(2,1)S(1)} %collective-permute-done.21.refs_2_, ...), custom_call_target="tpu_custom_call" | custom-call | flops 629145600 | bytes 9830400 | tf_op jit(solution)/shard_map/pallas_call | solution.py:552
  45.6 2.5 %shard_map.64 = (f32[32,16,128]{2,1,0:T(8,128)S(1)}, f32[32,16,128]{2,1,0:T(8,128)S(1)}, f32[8,16,128]{2,1,0:T(8,128)S(1)}, f32[144,128]{1,0:T(8,128)S(1)}) custom-call(f32[144,128]{1,0:T(8,128)S(1)} %get-tuple-element.117.refs_0_, f32[144,128]{1,0:T(8,128)S(1)} %collective-permute-done.16.refs_1_, f32[144,128]{1,0:T(8,128)S(1)} %collective-permute-done.17.refs_2_, ...), custom_call_target="tpu_custom_call" | custom-call | flops 209715200 | bytes 3276800 | tf_op jit(solution)/shard_map/pallas_call | solution.py:562
  50.2 1.5 %collective-permute-start.25 = (f32[144,128]{1,0:T(8,128)S(1)}, f32[144,128]{1,0:T(8,128)S(1)}, u32[]{:S(2)}, u32[]{:S(2)}) collective-permute-start(f32[144,128]{1,0:T(8,128)S(1)} %get-tuple-element.130.refs_0_), channel_id=1, source_target_pairs={{0,24},{8,16},{16,8},{24,0},{1,25},{9,17},{17,9},{25,1},{2,26},{10... | collective-permute-start | bytes 221192 | tf_op jit(solution)/shard_map/ppermute | solution.py:458
  52.6 1.5 %collective-permute-done.24.refs_2_ = f32[144,128]{1,0:T(8,128)S(1)} collective-permute-done((f32[144,128]{1,0:T(8,128)S(1)}, f32[144,128]{1,0:T(8,128)S(1)}, u32[]{:S(2)}, u32[]{:S(2)}) %collective-permute-start.24) | collective-permute-done | bytes 73760 | tf_op jit(solution)/shard_map/ppermute | solution.py:458
  54.2 1.3 %collective-permute-done.25.refs_3_ = f32[144,128]{1,0:T(8,128)S(1)} collective-permute-done((f32[144,128]{1,0:T(8,128)S(1)}, f32[144,128]{1,0:T(8,128)S(1)}, u32[]{:S(2)}, u32[]{:S(2)}) %collective-permute-start.25) | collective-permute-done | bytes 73760 | tf_op jit(solution)/shard_map/ppermute | solution.py:458
  57.7 1.5 %collective-permute-start.29 = (f32[72,128]{1,0:T(8,128)S(1)}, f32[72,128]{1,0:T(8,128)S(1)}, u32[]{:S(2)}, u32[]{:S(2)}) collective-permute-start(f32[72,128]{1,0:T(8,128)S(1)} %get-tuple-element.135), channel_id=1, source_target_pairs={{0,6},{1,7},{2,4},{3,5},{4,2},{5,3},{6,0},{7,1},{8,14},{9,15},{10,... | collective-permute-start | bytes 110600 | tf_op jit(solution)/shard_map/ppermute | solution.py:458
  59.2 4.4 %collective-permute-done.27.refs_1_ = f32[144,128]{1,0:T(8,128)S(1)} collective-permute-done((f32[144,128]{1,0:T(8,128)S(1)}, f32[144,128]{1,0:T(8,128)S(1)}, u32[]{:S(2)}, u32[]{:S(2)}) %collective-permute-start.27) | collective-permute-done | bytes 73760 | tf_op jit(solution)/shard_map/ppermute | solution.py:545
  68.2 1.4 %collective-permute-start.33 = (f32[32,4,128]{2,1,0:T(4,128)S(1)}, f32[32,4,128]{2,1,0:T(4,128)S(1)}, u32[]{:S(2)}, u32[]{:S(2)}) collective-permute-start(f32[32,4,128]{2,1,0:T(4,128)S(1)} %get-tuple-element.142), channel_id=1, source_target_pairs={{0,24},{8,16},{16,8},{24,0},{1,25},{9,17},{17,9},{25,1},{2,26},{10... | collective-permute-start | bytes 196616 | tf_op jit(solution)/shard_map/ppermute | solution.py:458
  71.2 2.1 %collective-permute-done.33.refs_3_ = f32[32,4,128]{2,1,0:T(4,128)S(1)} collective-permute-done((f32[32,4,128]{2,1,0:T(4,128)S(1)}, f32[32,4,128]{2,1,0:T(4,128)S(1)}, u32[]{:S(2)}, u32[]{:S(2)}) %collective-permute-start.33) | collective-permute-done | bytes 65568 | tf_op jit(solution)/shard_map/ppermute | solution.py:458
  (48 shorter events, 18.6 us)
Async XLA Ops:
  4.6 9.0 %collective-permute-start.6 = (bf16[784,128]{1,0:T(8,128)(2,1)S(1)}, bf16[784,128]{1,0:T(8,128)(2,1)S(1)}, u32[]{:S(2)}, u32[]{:S(2)}) collective-permute-start(bf16[784,128]{1,0:T(8,128)(2,1)S(1)} %get-tuple-element.92), channel_id=1, source_target_pairs={{0,8},{8,0},{16,24},{24,16},{1,9},{9,1},{17,25},{25,17},{2,10},{10... | collective-permute-start | bytes 602120 | tf_op jit(solution)/shard_map/ppermute | solution.py:458
  7.6 10.7 %collective-permute-start.7 = (bf16[784,128]{1,0:T(8,128)(2,1)S(1)}, bf16[784,128]{1,0:T(8,128)(2,1)S(1)}, u32[]{:S(2)}, u32[]{:S(2)}) collective-permute-start(bf16[784,128]{1,0:T(8,128)(2,1)S(1)} %get-tuple-element.93), channel_id=1, source_target_pairs={{0,16},{8,24},{16,0},{24,8},{1,17},{9,25},{17,1},{25,9},{2,18},{10... | collective-permute-start | bytes 602120 | tf_op jit(solution)/shard_map/ppermute | solution.py:458
  9.1 9.2 %collective-permute-start.8 = (bf16[784,128]{1,0:T(8,128)(2,1)S(1)}, bf16[784,128]{1,0:T(8,128)(2,1)S(1)}, u32[]{:S(2)}, u32[]{:S(2)}) collective-permute-start(bf16[784,128]{1,0:T(8,128)(2,1)S(1)} %get-tuple-element.94), channel_id=1, source_target_pairs={{0,24},{8,16},{16,8},{24,0},{1,25},{9,17},{17,9},{25,1},{2,26},{10... | collective-permute-start | bytes 602120 | tf_op jit(solution)/shard_map/ppermute | solution.py:458
  10.2 10.0 %collective-permute-start.10 = (f32[32,4,128]{2,1,0:T(4,128)S(1)}, f32[32,4,128]{2,1,0:T(4,128)S(1)}, u32[]{:S(2)}, u32[]{:S(2)}) collective-permute-start(f32[32,4,128]{2,1,0:T(4,128)S(1)} %get-tuple-element.111), channel_id=1, source_target_pairs={{0,16},{8,24},{16,0},{24,8},{1,17},{9,25},{17,1},{25,9},{2,18},{10... | collective-permute-start | bytes 196616 | tf_op jit(solution)/shard_map/ppermute | solution.py:458
  12.3 7.9 %collective-permute-start.11 = (f32[32,4,128]{2,1,0:T(4,128)S(1)}, f32[32,4,128]{2,1,0:T(4,128)S(1)}, u32[]{:S(2)}, u32[]{:S(2)}) collective-permute-start(f32[32,4,128]{2,1,0:T(4,128)S(1)} %get-tuple-element.112), channel_id=1, source_target_pairs={{0,24},{8,16},{16,8},{24,0},{1,25},{9,17},{17,9},{25,1},{2,26},{10... | collective-permute-start | bytes 196616 | tf_op jit(solution)/shard_map/ppermute | solution.py:458
  13.6 6.6 %collective-permute-start.9 = (f32[32,4,128]{2,1,0:T(4,128)S(1)}, f32[32,4,128]{2,1,0:T(4,128)S(1)}, u32[]{:S(2)}, u32[]{:S(2)}) collective-permute-start(f32[32,4,128]{2,1,0:T(4,128)S(1)} %get-tuple-element.110), channel_id=1, source_target_pairs={{0,8},{8,0},{16,24},{24,16},{1,9},{9,1},{17,25},{25,17},{2,10},{10... | collective-permute-start | bytes 196616 | tf_op jit(solution)/shard_map/ppermute | solution.py:458
  21.0 5.4 %collective-permute-start.12 = (f32[144,128]{1,0:T(8,128)S(1)}, f32[144,128]{1,0:T(8,128)S(1)}, u32[]{:S(2)}, u32[]{:S(2)}) collective-permute-start(f32[144,128]{1,0:T(8,128)S(1)} %get-tuple-element.114.refs_0_), channel_id=1, source_target_pairs={{0,8},{8,0},{16,24},{24,16},{1,9},{9,1},{17,25},{25,17},{2,10},{10... | collective-permute-start | bytes 221192 | tf_op jit(solution)/shard_map/ppermute | solution.py:458
  21.4 6.6 %collective-permute-start.13 = (f32[144,128]{1,0:T(8,128)S(1)}, f32[144,128]{1,0:T(8,128)S(1)}, u32[]{:S(2)}, u32[]{:S(2)}) collective-permute-start(f32[144,128]{1,0:T(8,128)S(1)} %get-tuple-element.114.refs_0_), channel_id=1, source_target_pairs={{0,16},{8,24},{16,0},{24,8},{1,17},{9,25},{17,1},{25,9},{2,18},{10... | collective-permute-start | bytes 221192 | tf_op jit(solution)/shard_map/ppermute | solution.py:458
  22.9 5.5 %collective-permute-start.14 = (f32[144,128]{1,0:T(8,128)S(1)}, f32[144,128]{1,0:T(8,128)S(1)}, u32[]{:S(2)}, u32[]{:S(2)}) collective-permute-start(f32[144,128]{1,0:T(8,128)S(1)} %get-tuple-element.114.refs_0_), channel_id=1, source_target_pairs={{0,24},{8,16},{16,8},{24,0},{1,25},{9,17},{17,9},{25,1},{2,26},{10... | collective-permute-start | bytes 221192 | tf_op jit(solution)/shard_map/ppermute | solution.py:458
  24.5 19.7 %collective-permute-start.20 = (bf16[768,128]{1,0:T(8,128)(2,1)S(1)}, bf16[768,128]{1,0:T(8,128)(2,1)S(1)}, u32[]{:S(2)}, u32[]{:S(2)}) collective-permute-start(bf16[768,128]{1,0:T(8,128)(2,1)S(1)} %get-tuple-element.122), channel_id=1, source_target_pairs={{0,8},{8,0},{16,24},{24,16},{1,9},{9,1},{17,25},{25,17},{2,10},{10... | collective-permute-start | bytes 589832 | tf_op jit(solution)/shard_map/ppermute | solution.py:458
  24.8 19.3 %collective-permute-start.21 = (bf16[768,128]{1,0:T(8,128)(2,1)S(1)}, bf16[768,128]{1,0:T(8,128)(2,1)S(1)}, u32[]{:S(2)}, u32[]{:S(2)}) collective-permute-start(bf16[768,128]{1,0:T(8,128)(2,1)S(1)} %get-tuple-element.123), channel_id=1, source_target_pairs={{0,16},{8,24},{16,0},{24,8},{1,17},{9,25},{17,1},{25,9},{2,18},{10... | collective-permute-start | bytes 589832 | tf_op jit(solution)/shard_map/ppermute | solution.py:458
  26.4 17.7 %collective-permute-start.22 = (bf16[768,128]{1,0:T(8,128)(2,1)S(1)}, bf16[768,128]{1,0:T(8,128)(2,1)S(1)}, u32[]{:S(2)}, u32[]{:S(2)}) collective-permute-start(bf16[768,128]{1,0:T(8,128)(2,1)S(1)} %get-tuple-element.124), channel_id=1, source_target_pairs={{0,24},{8,16},{16,8},{24,0},{1,25},{9,17},{17,9},{25,1},{2,26},{10... | collective-permute-start | bytes 589832 | tf_op jit(solution)/shard_map/ppermute | solution.py:458
  29.0 7.7 %collective-permute-start.15 = (f32[144,128]{1,0:T(8,128)S(1)}, f32[144,128]{1,0:T(8,128)S(1)}, u32[]{:S(2)}, u32[]{:S(2)}) collective-permute-start(f32[144,128]{1,0:T(8,128)S(1)} %get-tuple-element.115.own_ref), channel_id=1, source_target_pairs={{0,1},{1,0},{2,3},{3,2},{4,5},{5,4},{6,7},{7,6},{8,9},{9,8},{10,11... | collective-permute-start | bytes 221192 | tf_op jit(solution)/shard_map/ppermute | solution.py:458
  36.9 6.0 %collective-permute-start.16 = (f32[144,128]{1,0:T(8,128)S(1)}, f32[144,128]{1,0:T(8,128)S(1)}, u32[]{:S(2)}, u32[]{:S(2)}) collective-permute-start(f32[144,128]{1,0:T(8,128)S(1)} %get-tuple-element.118), channel_id=1, source_target_pairs={{0,2},{1,5},{2,0},{3,7},{4,6},{5,1},{6,4},{7,3},{8,10},{9,13},{10,... | collective-permute-start | bytes 221192 | tf_op jit(solution)/shard_map/ppermute | solution.py:545
  37.0 6.6 %collective-permute-start.18 = (f32[72,128]{1,0:T(8,128)S(1)}, f32[72,128]{1,0:T(8,128)S(1)}, u32[]{:S(2)}, u32[]{:S(2)}) collective-permute-start(f32[72,128]{1,0:T(8,128)S(1)} %get-tuple-element.119), channel_id=1, source_target_pairs={{0,6},{1,7},{2,4},{3,5},{4,2},{5,3},{6,0},{7,1},{8,14},{9,15},{10,... | collective-permute-start | bytes 110600 | tf_op jit(solution)/shard_map/ppermute | solution.py:458
  42.9 2.7 %collective-permute-start.17 = (f32[144,128]{1,0:T(8,128)S(1)}, f32[144,128]{1,0:T(8,128)S(1)}, u32[]{:S(2)}, u32[]{:S(2)}) collective-permute-start(f32[144,128]{1,0:T(8,128)S(1)} %collective-permute-done.16.refs_1_), channel_id=1, source_target_pairs={{0,1},{1,0},{2,3},{3,2},{4,5},{5,4},{6,7},{7,6},{8,9},{9,8},{10,11... | collective-permute-start | bytes 221192 | tf_op jit(solution)/shard_map/ppermute | solution.py:458
  48.2 4.5 %collective-permute-start.23 = (f32[144,128]{1,0:T(8,128)S(1)}, f32[144,128]{1,0:T(8,128)S(1)}, u32[]{:S(2)}, u32[]{:S(2)}) collective-permute-start(f32[144,128]{1,0:T(8,128)S(1)} %get-tuple-element.130.refs_0_), channel_id=1, source_target_pairs={{0,8},{8,0},{16,24},{24,16},{1,9},{9,1},{17,25},{25,17},{2,10},{10... | collective-permute-start | bytes 221192 | tf_op jit(solution)/shard_map/ppermute | solution.py:458
  49.0 5.1 %collective-permute-start.24 = (f32[144,128]{1,0:T(8,128)S(1)}, f32[144,128]{1,0:T(8,128)S(1)}, u32[]{:S(2)}, u32[]{:S(2)}) collective-permute-start(f32[144,128]{1,0:T(8,128)S(1)} %get-tuple-element.130.refs_0_), channel_id=1, source_target_pairs={{0,16},{8,24},{16,0},{24,8},{1,17},{9,25},{17,1},{25,9},{2,18},{10... | collective-permute-start | bytes 221192 | tf_op jit(solution)/shard_map/ppermute | solution.py:458
  50.2 5.3 %collective-permute-start.25 = (f32[144,128]{1,0:T(8,128)S(1)}, f32[144,128]{1,0:T(8,128)S(1)}, u32[]{:S(2)}, u32[]{:S(2)}) collective-permute-start(f32[144,128]{1,0:T(8,128)S(1)} %get-tuple-element.130.refs_0_), channel_id=1, source_target_pairs={{0,24},{8,16},{16,8},{24,0},{1,25},{9,17},{17,9},{25,1},{2,26},{10... | collective-permute-start | bytes 221192 | tf_op jit(solution)/shard_map/ppermute | solution.py:458
  57.6 6.0 %collective-permute-start.27 = (f32[144,128]{1,0:T(8,128)S(1)}, f32[144,128]{1,0:T(8,128)S(1)}, u32[]{:S(2)}, u32[]{:S(2)}) collective-permute-start(f32[144,128]{1,0:T(8,128)S(1)} %get-tuple-element.134), channel_id=1, source_target_pairs={{0,2},{1,5},{2,0},{3,7},{4,6},{5,1},{6,4},{7,3},{8,10},{9,13},{10,... | collective-permute-start | bytes 221192 | tf_op jit(solution)/shard_map/ppermute | solution.py:545
  57.7 5.9 %collective-permute-start.29 = (f32[72,128]{1,0:T(8,128)S(1)}, f32[72,128]{1,0:T(8,128)S(1)}, u32[]{:S(2)}, u32[]{:S(2)}) collective-permute-start(f32[72,128]{1,0:T(8,128)S(1)} %get-tuple-element.135), channel_id=1, source_target_pairs={{0,6},{1,7},{2,4},{3,5},{4,2},{5,3},{6,0},{7,1},{8,14},{9,15},{10,... | collective-permute-start | bytes 110600 | tf_op jit(solution)/shard_map/ppermute | solution.py:458
  66.1 4.4 %collective-permute-start.31 = (f32[32,4,128]{2,1,0:T(4,128)S(1)}, f32[32,4,128]{2,1,0:T(4,128)S(1)}, u32[]{:S(2)}, u32[]{:S(2)}) collective-permute-start(f32[32,4,128]{2,1,0:T(4,128)S(1)} %get-tuple-element.140), channel_id=1, source_target_pairs={{0,8},{8,0},{16,24},{24,16},{1,9},{9,1},{17,25},{25,17},{2,10},{10... | collective-permute-start | bytes 196616 | tf_op jit(solution)/shard_map/ppermute | solution.py:458
  66.9 4.3 %collective-permute-start.32 = (f32[32,4,128]{2,1,0:T(4,128)S(1)}, f32[32,4,128]{2,1,0:T(4,128)S(1)}, u32[]{:S(2)}, u32[]{:S(2)}) collective-permute-start(f32[32,4,128]{2,1,0:T(4,128)S(1)} %get-tuple-element.141), channel_id=1, source_target_pairs={{0,16},{8,24},{16,0},{24,8},{1,17},{9,25},{17,1},{25,9},{2,18},{10... | collective-permute-start | bytes 196616 | tf_op jit(solution)/shard_map/ppermute | solution.py:458
  68.2 5.2 %collective-permute-start.33 = (f32[32,4,128]{2,1,0:T(4,128)S(1)}, f32[32,4,128]{2,1,0:T(4,128)S(1)}, u32[]{:S(2)}, u32[]{:S(2)}) collective-permute-start(f32[32,4,128]{2,1,0:T(4,128)S(1)} %get-tuple-element.142), channel_id=1, source_target_pairs={{0,24},{8,16},{16,8},{24,0},{1,25},{9,17},{17,9},{25,1},{2,26},{10... | collective-permute-start | bytes 196616 | tf_op jit(solution)/shard_map/ppermute | solution.py:458
  (4 other events, 6.1 us)
